TPU v7x, 512 devices: a whole 4x4x16 slice. The times are simulated.
512 devices in a mesh: ctx: 32 (over z, y_lo), tp: 16 (over y_hi, x, core).
Axes of the slice: x: 4, y: 4 (y_hi: 2, y_lo: 2; y = y_hi * 2 + y_lo), z: 16, core: 2. Of those that a mesh axis runs over, the one named last changes fastest.
Arguments:
- gate_in: bfloat16 [4096, 4096], P('ctx', 'tp'), may hold values from -250 to 250, as said below
- conv_in: bfloat16 [4096, 4096], P('ctx', 'tp'), may hold values from -6 to 6
- value_in: bfloat16 [4096, 4096], P('ctx', 'tp'), may hold values from -6 to 6
- filter_taps: float32 [128, 4096], P(None, 'tp'), may hold values from -0.5 to 0.5
- norm_gain: float32 [4096], P('tp'), may hold values from 0.1 to 1.9
- qkv_weight: bfloat16 [4096, 3, 2048], P(None, None, 'tp'), may hold values from -0.5 to 0.5
Outputs:
- attended: bfloat16 [4096, 2048], P('ctx', 'tp')
Inputs may be any that keep to these rules, and one draw needn't show every extreme that they name: `gate_in`: gate values; channels and bases carry different scales.
All inputs are finite; a program needn't handle non-finite values.
Results may differ from a plain program's by a relative error of at most 0.027.
Values may be sent and summed in bfloat16 or wider, within the bound.
A program may use at most 128 MiB of HBM per device.

v0:
```python
import math

import jax
import jax.numpy as jnp
from jax import lax
from jax.sharding import PartitionSpec as P

D = 4096
HEAD_DIM = 128


def passed_along(value, axis, by):
    devices = lax.axis_size(axis)
    pairs = [(i, i + by) for i in range(devices) if 0 <= i + by < devices]
    return lax.ppermute(value, axis, pairs)


def causal_filter(full, taps):
    span = taps.shape[0]
    channels = full.shape[1]
    stride = math.gcd(span, 32)
    reach_count = span // stride
    out_blocks = (full.shape[0] - span) // stride
    blocks = full.reshape(full.shape[0] // stride, stride, channels)
    windows = jnp.stack(
        [blocks[offset : offset + out_blocks] for offset in range(reach_count + 1)], axis=0
    )
    within = jnp.arange(stride, dtype=jnp.int32)
    block_start = jnp.arange(reach_count + 1, dtype=jnp.int32) * stride
    tap_index = span + within[None, :, None] - block_start[:, None, None] - within[None, None, :]
    valid = (tap_index >= 0) & (tap_index < span)
    weights_table = jnp.where(valid[:, :, :, None], taps[jnp.clip(tap_index, 0, span - 1)], 0.0)
    result = jnp.einsum("mksc,misc->kic", windows, weights_table, precision=lax.Precision.HIGHEST)
    return result.reshape(out_blocks * stride, channels)


def body(gate_in, conv_in, value_in, filter_taps, norm_gain, qkv_weight):
    rows = gate_in.shape[0]
    taps = filter_taps.shape[0]
    channels = gate_in.shape[1]
    mixed = (conv_in.astype(jnp.float32) * value_in.astype(jnp.float32)).astype(jnp.bfloat16)
    rim = passed_along(mixed[rows - (taps - 1) :], "ctx", 1)
    full = jnp.concatenate([jnp.zeros((1, channels), jnp.bfloat16), rim, mixed], axis=0).astype(
        jnp.float32
    )
    filtered = causal_filter(full, filter_taps)
    hyena = (gate_in.astype(jnp.float32) * filtered).astype(jnp.bfloat16).astype(jnp.float32)
    squares = jnp.sum(hyena * hyena, axis=1)
    summed = lax.psum(squares, "tp")
    normed = (hyena * lax.rsqrt(summed / D + 1e-06)[:, None] * norm_gain[None, :]).astype(
        jnp.bfloat16
    )
    width = qkv_weight.shape[2]
    heads_here = width // HEAD_DIM
    flat = qkv_weight.reshape(qkv_weight.shape[0], 3 * width)
    proj = jnp.dot(
        lax.all_gather(normed, "tp", axis=1, tiled=True), flat, preferred_element_type=jnp.float32
    )
    proj = proj.astype(jnp.bfloat16).reshape(rows, 3, heads_here, HEAD_DIM)
    query = proj[:, 0]
    keys = proj[:, 1]
    values = proj[:, 2]
    index = lax.axis_index("ctx")
    half = rows // 2
    local = jnp.arange(rows, dtype=jnp.int32)
    positions = index * rows + local
    scale = 1.0 / math.sqrt(HEAD_DIM)
    start = jnp.int32(0)
    key_piece = lax.all_gather(keys, "ctx", axis=0, tiled=True)
    value_piece = lax.all_gather(values, "ctx", axis=0, tiled=True)
    key_pos = jnp.arange(key_piece.shape[0], dtype=jnp.int32)
    running_max = jnp.full((rows, heads_here), -1e30, jnp.float32)
    running_total = jnp.zeros((rows, heads_here), jnp.float32)
    running_acc = jnp.zeros((rows, heads_here, HEAD_DIM), jnp.float32)
    outputs = []
    for which in range(2):
        lower = which * half
        qpart = query[lower : lower + half]
        qpos = positions[lower : lower + half]
        state = (
            running_max[lower : lower + half],
            running_total[lower : lower + half],
            running_acc[lower : lower + half],
        )

        def compute(state):
            old_max, old_total, old_acc = state
            scores = (
                jnp.einsum("qhd,khd->hqk", qpart, key_piece, preferred_element_type=jnp.float32)
                * scale
            )
            allowed = (qpos[:, None] >= key_pos[None, :])[None]
            scores = jnp.where(allowed, scores, -1e30)
            new_max = jnp.maximum(old_max, jnp.max(scores, axis=2).T)
            expo = jnp.where(allowed, jnp.exp(scores - new_max.T[:, :, None]), 0.0)
            new_total = jnp.sum(expo, axis=2).T
            weights = expo.astype(jnp.bfloat16)
            added = jnp.einsum(
                "hqk,khd->qhd", weights, value_piece, preferred_element_type=jnp.float32
            )
            return (new_max, new_total, added)

        def keep(state):
            return state

        outputs.append(lax.cond(start <= jnp.max(qpos), compute, keep, state))
    final_max, final_total, final_acc = tuple(
        (jnp.concatenate([outputs[0][slot], outputs[1][slot]], axis=0) for slot in range(3))
    )
    attended = (final_acc / final_total[:, :, None]).astype(jnp.bfloat16).reshape(rows, width)
    return attended


def solution(mesh):
    placed = (
        P("ctx", "tp"),
        P("ctx", "tp"),
        P("ctx", "tp"),
        P(None, "tp"),
        P("tp"),
        P(None, None, "tp"),
    )
    return jax.shard_map(
        body, mesh=mesh, in_specs=placed, out_specs=P("ctx", "tp"), check_vma=False
    )
```

profile of v0, /device:TPU:28, one launch (start us, length us, event | category | flops | bytes accessed | tf_op | source)
XLA Modules:
  0.0 438.2 jit_solution(1505640722404212542)
XLA Ops:
  6.5 0.9 multiply_convert_fusion
  7.5 4.0 collective-permute-start
  11.9 20.0 %gather_fusion = f32[5120,256]{1,0:T(8,128)} fusion(f32[128,256]{1,0:T(8,128)S(1)} %copy-done, s32[5120]{0:T(1024)S(1)} %broadcast_clamp_fusion), kind=kCustom, calls=%fused_computation | custom fusion | bytes 10506240 | tf_op jit(solution)/shard_map/gather | solution.py:32
  31.9 17.4 %copy.31 = f32[5,32,32,256]{2,1,0,3:T(8,128)} copy(f32[5,32,32,256]{3,2,1,0:T(8,128)} %bitcast.61) | data formatting | bytes 10485760 | tf_op jit(solution)/shard_map/gather | solution.py:32
  49.6 1.1 copy.32
  50.7 25.0 %fusion.28 = f32[4,32,256]{1,0,2:T(4,128)S(1)} fusion(f32[5,4,32,256]{2,1,0,3:T(4,128)S(1)} %copy.32, f32[5,32,32,256]{2,1,0,3:T(8,128)} %copy.31, pred[5,32,32]{2,1,0:T(8,128)(4,1)S(1)} %fusion.37), kind=kOutput, calls=%fused_computation.35 | convolution fusion | flops 64225280 | bytes 6034432 | tf_op jit(solution)/shard_map/mksc,misc->kic/dot_general | solution.py:33
  76.0 24.8 %psum.7 = f32[128]{0:T(128)S(1)} all-reduce(f32[128]{0:T(128)S(1)} %fusion.31), channel_id=1, replica_groups=mesh['ctx'=32,'tp'=16] {'tp'}, use_global_device_ids=true, to_apply=%region_2.3 | all-reduce | flops 128 | bytes 1024 | tf_op jit(solution)/shard_map/psum | solution.py:49
  100.8 0.7 fusion.33
  101.6 3.2 copy.34
  104.8 65.7 %all-gather.6.cloned.1.call-done = bf16[128,4096]{1,0:T(8,128)(2,1)} async-done(((bf16[128,256]{1,0:T(8,128)(2,1)}), bf16[128,4096]{1,0:T(8,128)(2,1)}) %all-gather.6.cloned.1.call-update) | async-done | bytes 1048592 | tf_op jit(solution)/shard_map/all_gather | solution.py:57
  170.5 2.3 convolution_convert_fusion
  172.9 0.6 fusion.43
  173.6 0.7 all-gather.10.cloned.1.call-update
  174.3 0.7 slice_reduce_fusion.1
  176.1 126.2 %all-gather.8.cloned.1.call-done = bf16[4096,1,1,128]{0,3,1,2:T(8,128)(2,1)} async-done(((bf16[128,1,1,128]{0,3,1,2:T(8,128)(2,1)}), bf16[4096,1,1,128]{0,3,1,2:T(8,128)(2,1)}) %all-gather.8.cloned.1.call-update) | async-done | bytes 1048592 | tf_op jit(solution)/shard_map/all_gather | solution.py:69
  302.3 1.6 copy.36
  304.0 122.3 %all-gather.10.cloned.1.call-done = bf16[4096,1,1,128]{0,3,1,2:T(8,128)(2,1)} async-done(((bf16[128,1,1,128]{0,3,1,2:T(8,128)(2,1)}), bf16[4096,1,1,128]{0,3,1,2:T(8,128)(2,1)}) %all-gather.10.cloned.1.call-update) | async-done | bytes 1048592 | tf_op jit(solution)/shard_map/all_gather | solution.py:70
  426.3 1.6 copy.37
  427.9 1.5 conditional.2
  428.1 0.6 fusion.40
  428.7 0.4 fusion.1
  429.4 1.5 conditional.3
  429.6 0.6 fusion.41
  431.0 0.7 fusion.38
  (43 shorter events, 2.6 us)
Async XLA Ops:
  6.5 5.4 %copy-start = (f32[128,256]{1,0:T(8,128)S(1)}, f32[128,256]{1,0:T(8,128)}, u32[]{:S(2)}) copy-start(f32[128,256]{1,0:T(8,128)} %param.13) | copy-start | bytes 393220
  6.5 163.9 %all-gather.6.cloned.1.call-start = ((), (), s32[]{:S(2)}) async-start(), calls=%async_computation | async-start | bytes 1114112 | tf_op jit(solution)/shard_map/all_gather | solution.py:57
  7.5 41.8 %collective-permute-start = (bf16[127,256]{1,0:T(8,128)(2,1)S(1)}, bf16[127,256]{1,0:T(8,128)(2,1)S(1)}, u32[]{:S(2)}, u32[]{:S(2)}) collective-permute-start(bf16[127,256]{1,0:T(8,128)(2,1)S(1)} %slice.62), channel_id=1, source_target_pairs={{0,16},{16,32},{32,48},{48,64},{64,80},{80,96},{96,112},{112,128},... | collective-permute-start | bytes 195080 | tf_op jit(solution)/shard_map/ppermute | solution.py:15
  50.7 25.2 %copy-start.1 = (bf16[128,256]{1,0:T(8,128)(2,1)S(1)}, bf16[128,256]{1,0:T(8,128)(2,1)}, u32[]{:S(2)}) copy-start(bf16[128,256]{1,0:T(8,128)(2,1)} %param.10) | copy-start | bytes 196612
  50.7 50.1 %copy-start.2 = (f32[256]{0:T(256)S(1)}, f32[256]{0:T(256)}, u32[]{:S(2)}) copy-start(f32[256]{0:T(256)} %param.14) | copy-start | bytes 3076
  101.5 200.8 %all-gather.8.cloned.1.call-start = ((), (), s32[]{:S(2)}) async-start(), calls=%async_computation.1 | async-start | bytes 1081344 | tf_op jit(solution)/shard_map/all_gather | solution.py:69
  173.5 252.7 %all-gather.10.cloned.1.call-start = ((), (), s32[]{:S(2)}) async-start(), calls=%async_computation.2 | async-start | bytes 1081344 | tf_op jit(solution)/shard_map/all_gather | solution.py:70
Sparse Core Ops, SparseCore 0:
  101.6 68.7 all-gather.5
  173.7 128.6 all-gather.7
  304.3 121.8 all-gather.9
where the time goes:
time: 439 us; the launch traced here: 438 us
  waiting for transfers between devices  315 us (72%)
  local copies, waits for them, and re-layouts  46.4 us (11%)
  matrix products  29.2 us (7%)
  blocking collectives  24.8 us (6%)
  between operations  14.5 us (3%)
    all_gather x1, waiting for transfers between devices, body(): key_piece = lax.all_gather(keys, 'ctx', axis=0, tiled=True)  126 us
    all_gather x1, waiting for transfers between devices, body(): value_piece = lax.all_gather(values, 'ctx', axis=0, tiled=True)  122 us
    all_gather x1, waiting for transfers between devices, body(): lax.all_gather(normed, 'tp', axis=1, tiled=True)  65.7 us
    gather x2, local copies, waits for them, and re-layouts, causal_filter(): taps[jnp.clip(tap_index, 0, span - 1)]  37.4 us
    dot_general x1, matrix products, causal_filter(): jnp.einsum('mksc,misc->kic', windows, weights_table, precision=lax.Precis...  25 us
    psum x1, blocking collectives, body(): summed = lax.psum(squares, 'tp')  24.8 us
  transfers between devices with their start and end apart: 4, of which 3 were waited for; matrix products, arithmetic and copies ran while one was open for 10% of the time, Pallas kernels for 0%

commit v1 on v0

v1 whole, which is shorter than its diff:
```python
import math

import jax
import jax.numpy as jnp
from jax import lax
from jax.experimental import pallas as pl
from jax.experimental.pallas import tpu as pltpu
from jax.sharding import PartitionSpec as P

D = 4096
HEAD_DIM = 128
ROWS = 128
CH = 256
CTX = 32
TP = 16
NZ = 16
NEAR = 3
F32 = jnp.float32
BF16 = jnp.bfloat16


def flipped(index, bits):
    out = index
    for bit in (1, 2, 4, 8):
        if bits & bit:
            out = out + bit - 2 * bit * ((index // bit) % 2)
    return out


def kernel(
    gate_ref, conv_ref, value_ref, taps_ref, gain_ref, w_hbm, out_ref,
    mixed, rim, shifted, xall, gains, w_ref, kv, q_ref, proj, squares,
    top, total, acc,
    w_sem, rim_send, rim_recv, gain_send, gain_recv,
    x_send, x_recv, half_send, half_recv, kv_send, kv_recv,
):
    c = lax.axis_index("ctx")
    tp = lax.axis_index("tp")
    z = c // 2
    partner = c + 1 - 2 * (c % 2)
    after = (c + 1) % CTX
    before = (c + CTX - 1) % CTX
    up = (c + 2) % CTX
    down = (c + CTX - 2) % CTX

    w_copy = pltpu.make_async_copy(w_hbm, w_ref, w_sem)
    w_copy.start()

    barrier = pltpu.get_barrier_semaphore()
    for bits in range(1, TP):
        pl.semaphore_signal(barrier, inc=1, device_id={"tp": flipped(tp, bits)})
    for other in (after, before, partner, up, down):
        pl.semaphore_signal(barrier, inc=1, device_id={"ctx": other})
    mixed[...] = (conv_ref[...].astype(F32) * value_ref[...].astype(F32)).astype(BF16)
    pl.semaphore_wait(barrier, TP - 1 + 5)

    sent = []

    def send(src, dst, send_sem, recv_sem, where):
        copy = pltpu.make_async_remote_copy(
            src_ref=src, dst_ref=dst, send_sem=send_sem, recv_sem=recv_sem, device_id=where
        )
        copy.start()
        sent.append(copy)

    def arrived(dst, send_sem, recv_sem, where):
        pltpu.make_async_remote_copy(
            src_ref=dst, dst_ref=dst, send_sem=send_sem, recv_sem=recv_sem, device_id=where
        ).wait_recv()

    send(mixed, rim, rim_send, rim_recv, {"ctx": after})
    for bits in range(1, TP):
        send(
            gain_ref, gains.at[bits], gain_send.at[bits], gain_recv.at[bits],
            {"tp": flipped(tp, bits)},
        )
    gains[0] = gain_ref[...]

    arrived(rim, rim_send, rim_recv, {"ctx": before})
    first = (c > 0).astype(F32)
    full = jnp.concatenate([rim[...].astype(F32) * first, mixed[...].astype(F32)], axis=0)
    for r in range(8):
        shifted[r] = full if r == 0 else pltpu.roll(full, r, 0)

    def tap_group(q, carry):
        base = pl.multiple_of(ROWS - 8 * q, 8)
        rows = taps_ref[pl.ds(pl.multiple_of(8 * q, 8), 8), :]
        for r in range(8):
            carry = carry + rows[r : r + 1, :] * shifted[r, pl.ds(base, ROWS), :]
        return carry

    filtered = lax.fori_loop(0, 16, tap_group, jnp.zeros((ROWS, CH), F32))
    xall[0] = (gate_ref[...].astype(F32) * filtered).astype(BF16)

    def push(slot, bits):
        send(
            xall.at[slot], xall.at[slot ^ bits], x_send.at[len(sent)], x_recv.at[slot ^ bits],
            {"tp": flipped(tp, bits)},
        )

    def push_half(slot, half, bits):
        rows = pl.ds(64 * half, 64)
        send(
            xall.at[slot, rows], xall.at[slot ^ bits, rows],
            half_send.at[slot // 8, half], half_recv.at[slot // 8, half],
            {"tp": flipped(tp, bits)},
        )

    def await_slot(slot):
        if slot % 8 == 4:
            for half in range(2):
                rows = xall.at[slot, pl.ds(64 * half, 64)]
                arrived(
                    rows, half_send.at[slot // 8, half], half_recv.at[slot // 8, half],
                    {"tp": flipped(tp, 2)},
                )
        else:
            arrived(xall.at[slot], x_send.at[0], x_recv.at[slot], {"tp": flipped(tp, 1)})

    def absorb(slot):
        h = xall[slot].astype(F32)
        squared = h * h
        part = squared[:, :128] + squared[:, 128:]
        squares[...] = part if slot == 0 else squares[...] + part
        x = (h * gains[slot]).astype(BF16)
        start = pl.multiple_of(flipped(tp, slot) * CH, CH)
        for i in range(3):
            added = jnp.dot(x, w_ref[i, pl.ds(start, CH), :], preferred_element_type=F32)
            proj[i] = added if slot == 0 else proj[i] + added

    for bits in (8, 2, 6, 1):
        push(0, bits)
    w_copy.wait()
    absorb(0)
    for bits in range(1, TP):
        arrived(gains.at[bits], gain_send.at[bits], gain_recv.at[bits], {"tp": flipped(tp, bits)})
    await_slot(1)
    absorb(1)
    await_slot(2)
    push_half(2, 0, 6)
    push(2, 1)
    await_slot(6)
    push_half(6, 1, 2)
    push(6, 1)
    absorb(2)
    absorb(6)
    await_slot(8)
    push(8, 2)
    push(8, 6)
    push(8, 1)
    await_slot(4)
    push(4, 1)
    absorb(8)
    absorb(4)
    await_slot(3)
    absorb(3)
    await_slot(7)
    absorb(7)
    await_slot(10)
    push_half(10, 0, 6)
    push(10, 1)
    await_slot(14)
    push_half(14, 1, 2)
    push(14, 1)
    absorb(10)
    absorb(14)
    await_slot(9)
    absorb(9)
    await_slot(5)
    absorb(5)
    await_slot(12)
    push(12, 1)
    absorb(12)
    for slot in (11, 15, 13):
        await_slot(slot)
        absorb(slot)

    msq = jnp.sum(squares[...], axis=1, keepdims=True) / D
    factor = lax.rsqrt(msq + 1e-06)
    kv[c] = jnp.concatenate([proj[1] * factor, proj[2] * factor], axis=1).astype(BF16)
    q_ref[...] = (proj[0] * factor).astype(BF16)

    counter = [0]

    def pass_on(source, direction, lane, step, other):
        send(
            kv.at[source], kv.at[source], kv_send.at[counter[0]],
            kv_recv.at[direction, lane, step], {"ctx": other},
        )
        counter[0] += 1

    def await_block(source, direction, lane, step):
        arrived(kv.at[source], kv_send.at[0], kv_recv.at[direction, lane, step], {"ctx": partner})

    def source_of(first_index, direction, step):
        move = CTX - 2 * step if direction == 0 else 2 * step
        return (first_index + move) % CTX

    row_pos = c * ROWS + lax.broadcasted_iota(jnp.int32, (ROWS, 256), 0)
    key_iota = lax.broadcasted_iota(jnp.int32, (ROWS, 256), 1)
    scale = 1.0 / math.sqrt(HEAD_DIM)

    def attend(z_source, initial=False):
        pair = kv[pl.ds(2 * z_source, 2)].reshape(256, 256)
        scores = (
            lax.dot_general(
                q_ref[...], pair[:, :128], (((1,), (1,)), ((), ())), preferred_element_type=F32
            )
            * scale
        )
        allowed = row_pos >= key_iota + z_source * 256
        scores = jnp.where(allowed, scores, -1e30)
        block_top = jnp.max(scores, axis=1, keepdims=True)
        new_top = block_top if initial else jnp.maximum(top[...], block_top)
        expo = jnp.where(allowed, jnp.exp(scores - new_top), 0.0)
        block_total = jnp.sum(expo, axis=1, keepdims=True)
        added = jnp.dot(expo.astype(BF16), pair[:, 128:], preferred_element_type=F32)
        if initial:
            total[...] = block_total
            acc[...] = added
        else:
            fade = jnp.exp(top[...] - new_top)
            total[...] = total[...] * fade + block_total
            acc[...] = acc[...] * fade + added
        top[...] = new_top

    def attend_step(step):
        @pl.when(z >= step)
        def _():
            attend((z + NZ - step) % NZ)

        if step < 8:
            @pl.when(z + step >= NZ)
            def _():
                attend((z + step) % NZ)

    toward = (up, down)
    last_a = (8, 7)
    pass_on(c, 0, 0, 1, up)
    pass_on(c, 1, 0, 1, down)
    pass_on(c, 0, 1, 0, partner)
    await_block(partner, 0, 1, 0)
    pass_on(partner, 0, 1, 1, up)
    pass_on(partner, 1, 1, 1, down)
    attend(z, initial=True)
    for step in range(1, 10):
        for direction in range(2):
            if step <= last_a[direction]:
                source = source_of(c, direction, step)
                await_block(source, direction, 0, step)
                if step < last_a[direction]:
                    pass_on(source, direction, 0, step + 1, toward[direction])
                if step > NEAR:
                    pass_on(source, direction, 1, step, partner)
        ready = step if step <= NEAR else step - 1
        if step == NEAR + 1:
            continue
        for direction in range(2):
            if ready <= last_a[direction]:
                source = source_of(partner, direction, ready)
                await_block(source, direction, 1, ready)
                if ready < NEAR:
                    pass_on(source, direction, 1, ready + 1, toward[direction])
        attend_step(ready)

    out_ref[...] = (acc[...] / total[...]).astype(BF16)
    for copy in sent:
        copy.wait_send()


def body(gate_in, conv_in, value_in, filter_taps, norm_gain, qkv_weight):
    vmem = pl.BlockSpec(memory_space=pltpu.VMEM)
    dma = pltpu.SemaphoreType.DMA
    return pl.pallas_call(
        kernel,
        out_shape=jax.ShapeDtypeStruct((ROWS, HEAD_DIM), BF16),
        in_specs=[vmem] * 5 + [pl.BlockSpec(memory_space=pl.ANY)],
        out_specs=vmem,
        scratch_shapes=[
            pltpu.VMEM((ROWS, CH), BF16),
            pltpu.VMEM((ROWS, CH), BF16),
            pltpu.VMEM((8, 2 * ROWS, CH), F32),
            pltpu.VMEM((TP, ROWS, CH), BF16),
            pltpu.VMEM((TP, 1, CH), F32),
            pltpu.VMEM((3, D, HEAD_DIM), BF16),
            pltpu.VMEM((CTX, ROWS, 2 * HEAD_DIM), BF16),
            pltpu.VMEM((ROWS, HEAD_DIM), BF16),
            pltpu.VMEM((3, ROWS, HEAD_DIM), F32),
            pltpu.VMEM((ROWS, HEAD_DIM), F32),
            pltpu.VMEM((ROWS, 1), F32),
            pltpu.VMEM((ROWS, 1), F32),
            pltpu.VMEM((ROWS, HEAD_DIM), F32),
            dma,
            dma,
            dma,
            dma((TP,)),
            dma((TP,)),
            dma((48,)),
            dma((TP,)),
            dma((2, 2)),
            dma((2, 2)),
            dma((48,)),
            dma((2, 2, 9)),
        ],
        compiler_params=pltpu.CompilerParams(collective_id=0, has_side_effects=True),
    )(
        gate_in, conv_in, value_in, filter_taps, norm_gain.reshape(1, CH),
        jnp.transpose(qkv_weight, (1, 0, 2)),
    )


def solution(mesh):
    placed = (
        P("ctx", "tp"),
        P("ctx", "tp"),
        P("ctx", "tp"),
        P(None, "tp"),
        P("tp"),
        P(None, None, "tp"),
    )
    return jax.shard_map(
        body, mesh=mesh, in_specs=placed, out_specs=P("ctx", "tp"), check_vma=False
    )
```

time: 439 us -> 71.6 us (0.16)
  the two profiles are of different devices: /device:TPU:28 before, /device:TPU:2 now
where the time goes in v1:
time: 71.6 us; the launch traced here: 71.4 us
  Pallas kernels  70.1 us (98%)
  local copies, waits for them, and re-layouts  1.38 us (2%)
    pallas_call x1, Pallas kernels, body(): pl.pallas_call(kernel, out_shape=jax.ShapeDtypeStruct((ROWS, HEAD_DIM), B...  70.1 us

profile of v1, /device:TPU:2, one launch (start us, length us, event | category | flops | bytes accessed | tf_op | source)
XLA Modules:
  0.0 71.4 jit_solution(15187206828646039610)
XLA Ops:
  0.0 70.1 %shard_map.64 = bf16[128,128]{1,0:T(8,128)(2,1)} custom-call(bf16[128,256]{1,0:T(8,128)(2,1)} %gate_ref.1, bf16[128,256]{1,0:T(8,128)(2,1)} %conv_ref.1, bf16[128,256]{1,0:T(8,128)(2,1)} %value_ref.1, f32[128,256]{1,0:T(8,128)} %taps_ref.1, f32[1,256]{1,0:T(1,128)} %bitcast.3, bf16[3,4096,128]{2,1,0:T(8,128)(2,1)} %bitcast.2), custom_call_target="tpu_custom_call" | custom-call | tf_op jit(solution)/shard_map/pallas_call | solution.py:274
  70.1 1.4 %copy.8 = bf16[128,128]{1,0:T(8,128)(2,1)} copy(bf16[128,128]{1,0:T(8,128)(2,1)} %shard_map.64) | data formatting | bytes 65536

commit v2 on v1

--- a/solution.py
+++ b/solution.py
@@ -14,7 +14,10 @@
 CTX = 32
 TP = 16
 NZ = 16
-NEAR = 3
+NEAR = 1
+PIECES = 2
+PARENT = {far: far - 1 for far in range(1, 9)}
+HOPS = sorted({far - near for far, near in PARENT.items()})
 F32 = jnp.float32
 BF16 = jnp.bfloat16
 
@@ -29,7 +32,7 @@
 
 def kernel(
     gate_ref, conv_ref, value_ref, taps_ref, gain_ref, w_hbm, out_ref,
-    mixed, rim, shifted, xall, gains, w_ref, kv, q_ref, proj, squares,
+    mixed, rim, shifted, filtered, xall, gains, w_ref, kv, q_ref, proj, squares,
     top, total, acc,
     w_sem, rim_send, rim_recv, gain_send, gain_recv,
     x_send, x_recv, half_send, half_recv, kv_send, kv_recv,
@@ -40,8 +43,10 @@
     partner = c + 1 - 2 * (c % 2)
     after = (c + 1) % CTX
     before = (c + CTX - 1) % CTX
-    up = (c + 2) % CTX
-    down = (c + CTX - 2) % CTX
+
+    def along(direction, hops):
+        return (c + (2 * hops if direction == 0 else CTX - 2 * hops)) % CTX
+
 
     w_copy = pltpu.make_async_copy(w_hbm, w_ref, w_sem)
     w_copy.start()
@@ -49,10 +54,11 @@
     barrier = pltpu.get_barrier_semaphore()
     for bits in range(1, TP):
         pl.semaphore_signal(barrier, inc=1, device_id={"tp": flipped(tp, bits)})
-    for other in (after, before, partner, up, down):
+    ringed = [along(direction, hops) for hops in HOPS for direction in range(2)]
+    for other in [after, before, partner] + ringed:
         pl.semaphore_signal(barrier, inc=1, device_id={"ctx": other})
     mixed[...] = (conv_ref[...].astype(F32) * value_ref[...].astype(F32)).astype(BF16)
-    pl.semaphore_wait(barrier, TP - 1 + 5)
+    pl.semaphore_wait(barrier, TP - 1 + 3 + 2 * len(HOPS))
 
     sent = []
 
@@ -76,21 +82,31 @@
         )
     gains[0] = gain_ref[...]
 
+    own = mixed[...].astype(F32)
+    for r in range(8):
+        shifted[r, pl.ds(ROWS, ROWS), :] = own if r == 0 else pltpu.roll(own, r, 0)
+
+    def tap_sum(q, start, count):
+        out = None
+        for r in range(8):
+            part = taps_ref[pl.ds(8 * q + r, 1), :] * shifted[r, pl.ds(start, count), :]
+            out = part if out is None else out + part
+        return out
+
+    filtered[...] = jnp.zeros((ROWS, CH), F32)
+    for q in range(15):
+        first = 8 * (q + 1)
+        filtered[pl.ds(first, ROWS - first), :] += tap_sum(q, ROWS + 8, ROWS - first)
+
     arrived(rim, rim_send, rim_recv, {"ctx": before})
-    first = (c > 0).astype(F32)
-    full = jnp.concatenate([rim[...].astype(F32) * first, mixed[...].astype(F32)], axis=0)
+    kept = (c > 0).astype(F32)
+    joined = jnp.concatenate([rim[...].astype(F32) * kept, own[:8]], axis=0)
     for r in range(8):
-        shifted[r] = full if r == 0 else pltpu.roll(full, r, 0)
-
-    def tap_group(q, carry):
-        base = pl.multiple_of(ROWS - 8 * q, 8)
-        rows = taps_ref[pl.ds(pl.multiple_of(8 * q, 8), 8), :]
-        for r in range(8):
-            carry = carry + rows[r : r + 1, :] * shifted[r, pl.ds(base, ROWS), :]
-        return carry
-
-    filtered = lax.fori_loop(0, 16, tap_group, jnp.zeros((ROWS, CH), F32))
-    xall[0] = (gate_ref[...].astype(F32) * filtered).astype(BF16)
+        shifted[r, pl.ds(0, ROWS + 8), :] = joined if r == 0 else pltpu.roll(joined, r, 0)
+    for q in range(16):
+        filtered[pl.ds(0, 8 * (q + 1)), :] += tap_sum(q, ROWS - 8 * q, 8 * (q + 1))
+
+    xall[0] = (gate_ref[...].astype(F32) * filtered[...]).astype(BF16)
 
     def push(slot, bits):
         send(
@@ -181,16 +197,19 @@
     q_ref[...] = (proj[0] * factor).astype(BF16)
 
     counter = [0]
-
-    def pass_on(source, direction, lane, step, other):
+    piece_rows = ROWS // PIECES
+
+    def pass_on(source, direction, lane, step, piece, other):
+        block = kv.at[source, pl.ds(piece * piece_rows, piece_rows)]
         send(
-            kv.at[source], kv.at[source], kv_send.at[counter[0]],
-            kv_recv.at[direction, lane, step], {"ctx": other},
+            block, block, kv_send.at[counter[0]],
+            kv_recv.at[direction, lane, step, piece], {"ctx": other},
         )
         counter[0] += 1
 
-    def await_block(source, direction, lane, step):
-        arrived(kv.at[source], kv_send.at[0], kv_recv.at[direction, lane, step], {"ctx": partner})
+    def await_block(source, direction, lane, step, piece):
+        block = kv.at[source, pl.ds(piece * piece_rows, piece_rows)]
+        arrived(block, kv_send.at[0], kv_recv.at[direction, lane, step, piece], {"ctx": partner})
 
     def source_of(first_index, direction, step):
         move = CTX - 2 * step if direction == 0 else 2 * step
@@ -234,33 +253,41 @@
             def _():
                 attend((z + step) % NZ)
 
-    toward = (up, down)
-    last_a = (8, 7)
-    pass_on(c, 0, 0, 1, up)
-    pass_on(c, 1, 0, 1, down)
-    pass_on(c, 0, 1, 0, partner)
-    await_block(partner, 0, 1, 0)
-    pass_on(partner, 0, 1, 1, up)
-    pass_on(partner, 1, 1, 1, down)
+    def spread(source, direction, lane, step, piece, limit):
+        for far in sorted(PARENT, reverse=True):
+            if PARENT[far] == step and far <= limit:
+                pass_on(source, direction, lane, far, piece, along(direction, far - step))
+
+    def last(direction, piece):
+        return 8 if (piece < (PIECES + 1) // 2) == (direction == 0) else 7
+
+    for piece in range(PIECES):
+        for direction in range(2):
+            spread(c, direction, 0, 0, piece, last(direction, piece))
+        pass_on(c, 0, 1, 0, piece, partner)
+    for piece in range(PIECES):
+        await_block(partner, 0, 1, 0, piece)
+        for direction in range(2):
+            spread(partner, direction, 1, 0, piece, NEAR)
     attend(z, initial=True)
     for step in range(1, 10):
-        for direction in range(2):
-            if step <= last_a[direction]:
-                source = source_of(c, direction, step)
-                await_block(source, direction, 0, step)
-                if step < last_a[direction]:
-                    pass_on(source, direction, 0, step + 1, toward[direction])
-                if step > NEAR:
-                    pass_on(source, direction, 1, step, partner)
+        for piece in range(PIECES):
+            for direction in range(2):
+                if step <= last(direction, piece):
+                    source = source_of(c, direction, step)
+                    await_block(source, direction, 0, step, piece)
+                    spread(source, direction, 0, step, piece, last(direction, piece))
+                    if step > NEAR:
+                        pass_on(source, direction, 1, step, piece, partner)
         ready = step if step <= NEAR else step - 1
         if step == NEAR + 1:
             continue
-        for direction in range(2):
-            if ready <= last_a[direction]:
-                source = source_of(partner, direction, ready)
-                await_block(source, direction, 1, ready)
-                if ready < NEAR:
-                    pass_on(source, direction, 1, ready + 1, toward[direction])
+        for piece in range(PIECES):
+            for direction in range(2):
+                if ready <= last(direction, piece):
+                    source = source_of(partner, direction, ready)
+                    await_block(source, direction, 1, ready, piece)
+                    spread(source, direction, 1, ready, piece, NEAR)
         attend_step(ready)
 
     out_ref[...] = (acc[...] / total[...]).astype(BF16)
@@ -280,6 +307,7 @@
             pltpu.VMEM((ROWS, CH), BF16),
             pltpu.VMEM((ROWS, CH), BF16),
             pltpu.VMEM((8, 2 * ROWS, CH), F32),
+            pltpu.VMEM((ROWS, CH), F32),
             pltpu.VMEM((TP, ROWS, CH), BF16),
             pltpu.VMEM((TP, 1, CH), F32),
             pltpu.VMEM((3, D, HEAD_DIM), BF16),
@@ -299,8 +327,8 @@
             dma((TP,)),
             dma((2, 2)),
             dma((2, 2)),
-            dma((48,)),
-            dma((2, 2, 9)),
+            dma((32 * PIECES,)),
+            dma((2, 2, 9, PIECES)),
         ],
         compiler_params=pltpu.CompilerParams(collective_id=0, has_side_effects=True),
     )(

time: 71.6 us -> 66.9 us (0.934)
  Pallas kernels: 70.1 us -> 65.3 us
    pallas_call x1, Pallas kernels: 70.1 us -> 65.3 us  [body(): pl.pallas_call(kernel, out_shape=jax.ShapeDtypeStruct((ROWS, HEAD_DIM), B...]
where the time goes in v2:
time: 66.9 us; the launch traced here: 66.7 us
  Pallas kernels  65.3 us (98%)
  local copies, waits for them, and re-layouts  1.38 us (2%)
    pallas_call x1, Pallas kernels, body(): pl.pallas_call(kernel, out_shape=jax.ShapeDtypeStruct((ROWS, HEAD_DIM), B...  65.3 us
    unnamed x1, local copies, waits for them, and re-layouts  1.38 us

profile of v2, /device:TPU:2, one launch (start us, length us, event | category | flops | bytes accessed | tf_op | source)
XLA Modules:
  0.0 66.7 jit_solution(7290189645302427162)
XLA Ops:
  0.0 65.3 %shard_map.64 = bf16[128,128]{1,0:T(8,128)(2,1)} custom-call(bf16[128,256]{1,0:T(8,128)(2,1)} %gate_ref.1, bf16[128,256]{1,0:T(8,128)(2,1)} %conv_ref.1, bf16[128,256]{1,0:T(8,128)(2,1)} %value_ref.1, f32[128,256]{1,0:T(8,128)} %taps_ref.1, f32[1,256]{1,0:T(1,128)} %bitcast.3, bf16[3,4096,128]{2,1,0:T(8,128)(2,1)} %bitcast.2), custom_call_target="tpu_custom_call" | custom-call | tf_op jit(solution)/shard_map/pallas_call | solution.py:301
  65.3 1.4 %copy.8 = bf16[128,128]{1,0:T(8,128)(2,1)} copy(bf16[128,128]{1,0:T(8,128)(2,1)} %shard_map.64) | data formatting | bytes 65536

commit v3 on v2

--- a/solution.py
+++ b/solution.py
@@ -123,7 +123,7 @@
         )
 
     def await_slot(slot):
-        if slot % 8 == 4:
+        if slot == 4:
             for half in range(2):
                 rows = xall.at[slot, pl.ds(64 * half, 64)]
                 arrived(
@@ -163,6 +163,7 @@
     await_slot(8)
     push(8, 2)
     push(8, 6)
+    push(8, 4)
     push(8, 1)
     await_slot(4)
     push(4, 1)
@@ -173,10 +174,8 @@
     await_slot(7)
     absorb(7)
     await_slot(10)
-    push_half(10, 0, 6)
     push(10, 1)
     await_slot(14)
-    push_half(14, 1, 2)
     push(14, 1)
     absorb(10)
     absorb(14)

time: 66.9 us -> 65.5 us (0.979)
  the two profiles are of different devices: /device:TPU:2 before, /device:TPU:32 now
where the time goes in v3:
time: 65.5 us; the launch traced here: 65.3 us
  Pallas kernels  63.9 us (98%)
  local copies, waits for them, and re-layouts  1.38 us (2%)
    pallas_call x1, Pallas kernels, body(): pl.pallas_call(kernel, out_shape=jax.ShapeDtypeStruct((ROWS, HEAD_DIM), B...  63.9 us
    unnamed x1, local copies, waits for them, and re-layouts  1.38 us

profile of v3, /device:TPU:32, one launch (start us, length us, event | category | flops | bytes accessed | tf_op | source)
XLA Modules:
  0.0 65.3 jit_solution(3559200045284878025)
XLA Ops:
  0.0 63.9 %shard_map.64 = bf16[128,128]{1,0:T(8,128)(2,1)} custom-call(bf16[128,256]{1,0:T(8,128)(2,1)} %gate_ref.1, bf16[128,256]{1,0:T(8,128)(2,1)} %conv_ref.1, bf16[128,256]{1,0:T(8,128)(2,1)} %value_ref.1, f32[128,256]{1,0:T(8,128)} %taps_ref.1, f32[1,256]{1,0:T(1,128)} %bitcast.3, bf16[3,4096,128]{2,1,0:T(8,128)(2,1)} %bitcast.2), custom_call_target="tpu_custom_call" | custom-call | tf_op jit(solution)/shard_map/pallas_call | solution.py:300
  63.9 1.4 %copy.8 = bf16[128,128]{1,0:T(8,128)(2,1)} copy(bf16[128,128]{1,0:T(8,128)(2,1)} %shard_map.64) | data formatting | bytes 65536
